TPU v7x, 32 devices: a whole 2x2x4 slice. The times are simulated.
32 devices in a mesh: dp: 8 (over z, core), tp: 4 (over y, x).
Axes of the slice: x: 2, y: 2, z: 4, core: 2. Of those that a mesh axis runs over, the one named last changes fastest.
Arguments:
- student_hidden: bfloat16 [1152, 3456], P('dp'), may hold values from -6 to 6
- norm_gain: float32 [3456], replicated, may hold values from 0.25 to 1.75
- projection: bfloat16 [3456, 8192], P(None, 'tp'), may hold values from -0.109375 to 0.109375
- teacher_partials: bfloat16 [4, 1152, 8192], P('tp', 'dp'), may hold values from -5 to 5
- teacher_residual: bfloat16 [1152, 8192], P('dp', 'tp'), may hold values from -90 to 90
- owner: int32 [1152], P('dp'), may hold values from 0 to 1151, as said below
Outputs:
- grad_scaled: float32 [3456, 8192], P('dp', 'tp')
Inputs may be any that keep to these rules, and one draw needn't show every extreme that they name: owner is a permutation of all token indices; the 144 teacher rows of each index of dp hold exactly 18 tokens owned by each index of dp.
All inputs are finite; a program needn't handle non-finite values.
Results may differ from a plain program's by a relative error of at most 0.009.
Values may be sent and summed in bfloat16 or wider, within the bound.
A program may use at most 128 MiB of HBM per device.

v0:
```python
import jax
import jax.numpy as jnp
from jax import lax
from jax.sharding import PartitionSpec as P


def agree(largest):
    return lax.pmax(largest, ("dp", "tp")) + 1e-06


def rounded_terms(partial_value, scale):
    return lax.optimization_barrier((partial_value / scale).astype(jnp.bfloat16)).astype(
        jnp.float32
    )


def per_device(student_hidden, norm_gain, projection, teacher_partials, teacher_residual, owner):
    columns = projection.shape[1]
    rows_dev = student_hidden.shape[0]
    terms_in = teacher_partials[0].astype(jnp.float32)
    summed_all = lax.psum(terms_in.astype(jnp.bfloat16), "tp").astype(jnp.float32)
    summed = lax.dynamic_slice_in_dim(summed_all, lax.axis_index("tp") * columns, columns, 1)
    teacher = (teacher_residual.astype(jnp.float32) + summed).astype(jnp.bfloat16)
    groups = lax.axis_size("dp")
    slots = rows_dev // groups
    destination = owner // rows_dev
    order = jnp.argsort(destination, stable=True)
    outgoing = teacher[order].reshape(groups, slots, columns)
    outgoing_owner = owner[order].reshape(groups, slots)
    arrived, arrived_owner = (
        lax.all_to_all(outgoing, "dp", split_axis=0, concat_axis=0, tiled=True),
        lax.all_to_all(outgoing_owner, "dp", split_axis=0, concat_axis=0, tiled=True),
    )
    placing = jnp.argsort(arrived_owner.reshape(-1) % rows_dev)
    target = arrived.reshape(rows_dev, columns)[placing]
    values = student_hidden.astype(jnp.float32)
    inverse = lax.rsqrt(jnp.mean(values * values, axis=-1, keepdims=True) + 1e-05)
    normed = (values * inverse * norm_gain).astype(jnp.bfloat16)
    pred = jnp.dot(normed, projection, preferred_element_type=jnp.float32)
    diff = (pred - target.astype(jnp.float32)).astype(jnp.bfloat16)
    feature_share = normed.shape[1] // groups
    blocks = lax.all_to_all(normed, "dp", split_axis=1, concat_axis=0, tiled=True).reshape(
        groups, rows_dev, feature_share
    )
    errors = lax.all_gather(diff, "dp", axis=0, tiled=True).reshape(groups, rows_dev, columns)
    partials = jnp.einsum("dsr,dsc->drc", blocks, errors, preferred_element_type=jnp.float32)
    scale = agree(jnp.max(jnp.abs(partials)))
    grad_scaled = jnp.sum(rounded_terms(partials, scale), axis=0)
    return grad_scaled


def solution(mesh):
    placed = (P("dp", None), P(), P(None, "tp"), P("tp", "dp", None), P("dp", "tp"), P("dp"))
    return jax.shard_map(
        per_device, mesh=mesh, in_specs=placed, out_specs=P("dp", "tp"), check_vma=False
    )
```

profile of v0, /device:TPU:0, one launch (start us, length us, event | category | flops | bytes accessed | tf_op | source)
XLA Modules:
  0.0 276.7 jit_solution(12854644300265450455)
XLA Ops:
  6.5 0.0 all-reduce.2.cloned.1.call-start
  6.5 0.7 all-reduce.2.cloned.1.call-update
  7.3 3.2 %sort.34 = (s32[144]{0:T(256)}, s32[144]{0:T(256)S(1)}) sort(s32[144]{0:T(256)S(1)} %and_select_fusion.1, s32[144]{0:T(256)S(1)} %iota.8), dimensions={0}, to_apply=%region_2.3 | sort | flops 1152 | bytes 2304 | tf_op jit(solution)/shard_map/jit(argsort)/sort | solution.py:27
  10.5 1.6 gather_fusion.1
  12.1 0.7 all_to_all.25
  12.8 6.4 %all-to-all-start.2 = ((s32[8,1,18]{2,1,0:T(1,128)}), s32[8,1,18]{2,1,0:T(1,128)S(1)}, u32[]{:S(2)}, u32[]{:S(2)}) async-start(s32[8,1,18]{2,1,0:T(1,128)} %all_to_all.25), calls=%async_computation.2 | async-start | bytes 8192 | tf_op jit(solution)/shard_map/all_to_all | solution.py:32
  19.1 0.3 fusion.1
  19.4 67.7 %all-reduce.2.cloned.1.call-done = bf16[144,8192]{1,0:T(8,128)(2,1)} async-done(((bf16[144,8192]{1,0:T(8,128)(2,1)}), bf16[144,8192]{1,0:T(8,128)(2,1)}) %all-reduce.2.cloned.1.call-update) | async-done | bytes 2359312 | tf_op jit(solution)/shard_map/psum | solution.py:21
  87.1 0.0 copy-done.2
  87.1 1.3 add_convert_fusion
  88.4 1.0 gather_fusion
  89.3 0.0 copy-start.3
  89.4 1.1 reshape.31
  90.4 0.0 all-to-all-done.2
  90.4 4.6 %all-to-all-start.1 = ((bf16[8,18,2048]{2,1,0:T(8,128)(2,1)}), bf16[8,18,2048]{2,1,0:T(8,128)(2,1)S(1)}, u32[]{:S(2)}, u32[]{:S(2)}) async-start(bf16[8,18,2048]{2,1,0:T(8,128)(2,1)} %reshape.31), calls=%async_computation.1 | async-start | bytes 1572864 | tf_op jit(solution)/shard_map/all_to_all | solution.py:31
  95.0 0.0 all-gather.2.cloned.1.call-start
  95.1 0.3 fusion.3
  95.4 0.1 rem.23
  95.5 3.2 %sort.35 = (s32[144]{0:T(256)}, s32[144]{0:T(256)S(1)}) sort(s32[144]{0:T(256)S(1)} %and_select_fusion, s32[144]{0:T(256)S(1)} %iota.9), dimensions={0}, to_apply=%region_3.4 | sort | flops 1152 | bytes 2304 | tf_op jit(solution)/shard_map/jit(argsort)/sort | solution.py:34
  98.7 17.2 %all-to-all-done.1 = bf16[8,18,2048]{2,1,0:T(8,128)(2,1)S(1)} async-done(((bf16[8,18,2048]{2,1,0:T(8,128)(2,1)}), bf16[8,18,2048]{2,1,0:T(8,128)(2,1)S(1)}, u32[]{:S(2)}, u32[]{:S(2)}) %all-to-all-start.1) | async-done | bytes 589856 | tf_op jit(solution)/shard_map/all_to_all | solution.py:31
  116.0 0.2 reshape.32
  116.2 1.0 gather_fusion.2
  117.1 8.4 %fusion = bf16[144,2048]{1,0:T(8,128)(2,1)} fusion(bf16[144,3456]{1,0:T(8,128)(2,1)S(1)} %fusion.3, bf16[3456,2048]{1,0:T(8,128)(2,1)} %param.8, bf16[144,2048]{1,0:T(8,128)(2,1)S(1)} %gather_fusion.2), kind=kOutput, calls=%fused_computation.9 | convolution fusion | flops 2039316480 | bytes 16330752 | tf_op jit(solution)/shard_map/dot_general | solution.py:39
  125.5 0.0 all-gather.2.cloned.1.call-update
  125.5 2.7 all_to_all.21
  128.2 0.4 copy.7
  128.6 63.4 %all_to_all.30 = bf16[144,8,432]{2,0,1:T(8,128)(2,1)S(1)} all-to-all(bf16[144,8,432]{2,0,1:T(8,128)(2,1)S(1)} %copy.7), channel_id=1, replica_groups=mesh['dp'=8,'tp'=4] {'dp'}, dimensions={1} | all-to-all | bytes 1990656 | tf_op jit(solution)/shard_map/all_to_all | solution.py:42
  192.0 7.9 %all-gather.2.cloned.1.call-done = bf16[1152,2048]{1,0:T(8,128)(2,1)} async-done(((bf16[144,2048]{1,0:T(8,128)(2,1)}), bf16[1152,2048]{1,0:T(8,128)(2,1)}) %all-gather.2.cloned.1.call-update) | async-done | bytes 4718608 | tf_op jit(solution)/shard_map/all_gather | solution.py:45
  199.9 16.4 %abs_reduce_fusion = (f32[]{:T(128)}, f32[8,432,2048]{2,1,0:T(8,128)}) fusion(bf16[8,144,2048]{2,1,0:T(8,128)(2,1)} %bitcast.10, bf16[144,8,432]{2,0,1:T(8,128)(2,1)S(1)} %all_to_all.30), kind=kOutput, calls=%fused_computation.5 | convolution fusion | flops 2052587520 | bytes 34025476 | tf_op jit(solution)/shard_map/dsr,dsc->drc/dot_general | solution.py:46
  216.2 37.0 %pmax.7 = f32[]{:T(128)} all-reduce(f32[]{:T(128)} %get-tuple-element.9), channel_id=1, replica_groups=mesh['dp'=8,'tp'=4] {'dp','tp'}, use_global_device_ids=true, to_apply=%region_5.6 | all-reduce | flops 1 | bytes 8 | tf_op jit(solution)/shard_map/pmax | solution.py:8
  253.9 11.1 %divide_convert_fusion = bf16[8,432,2048]{2,1,0:T(8,128)(2,1)S(1)} fusion(f32[8,432,2048]{2,1,0:T(8,128)} %get-tuple-element.10, f32[]{:T(128)S(6)} %add.43), kind=kLoop, calls=%fused_computation.4 | loop fusion | flops 14155776 | bytes 42467332 | tf_op jit(solution)/shard_map/convert_element_type | solution.py:12
  265.0 4.8 %convert_reduce_fusion = f32[432,2048]{1,0:T(8,128)} fusion(bf16[8,432,2048]{2,1,0:T(8,128)(2,1)S(1)} %divide_convert_fusion), kind=kLoop, calls=%fused_computation.3 | loop fusion | flops 13271040 | bytes 17694720 | tf_op jit(solution)/shard_map/reduce_sum | solution.py:48
  (16 shorter events, 0.1 us)
Async XLA Ops:
  6.5 0.7 copy-start
  6.5 12.6 %copy-start.1 = (bf16[144,3456]{1,0:T(8,128)(2,1)S(1)}, bf16[144,3456]{1,0:T(8,128)(2,1)}, u32[]{:S(2)}) copy-start(bf16[144,3456]{1,0:T(8,128)(2,1)} %param.6) | copy-start | bytes 2985988
  6.5 80.5 %copy-start.2 = (bf16[144,2048]{1,0:T(8,128)(2,1)S(1)}, bf16[144,2048]{1,0:T(8,128)(2,1)}, u32[]{:S(2)}) copy-start(bf16[144,2048]{1,0:T(8,128)(2,1)} %param.10) | copy-start | bytes 1769476
  6.5 80.5 %all-reduce.2.cloned.1.call-start = ((), (), s32[]{:S(2)}) async-start(), calls=%async_computation.3 | async-start | bytes 4718592 | tf_op jit(solution)/shard_map/psum | solution.py:21
  12.8 77.6 %all-to-all-start.2 = ((s32[8,1,18]{2,1,0:T(1,128)}), s32[8,1,18]{2,1,0:T(1,128)S(1)}, u32[]{:S(2)}, u32[]{:S(2)}) async-start(s32[8,1,18]{2,1,0:T(1,128)} %all_to_all.25), calls=%async_computation.2 | async-start | bytes 8192 | tf_op jit(solution)/shard_map/all_to_all | solution.py:32
  89.3 5.7 %copy-start.3 = (f32[3456]{0:T(1024)S(1)}, f32[3456]{0:T(1024)}, u32[]{:S(2)}) copy-start(f32[3456]{0:T(1024)} %param.7) | copy-start | bytes 41476
  90.4 25.6 %all-to-all-start.1 = ((bf16[8,18,2048]{2,1,0:T(8,128)(2,1)}), bf16[8,18,2048]{2,1,0:T(8,128)(2,1)S(1)}, u32[]{:S(2)}, u32[]{:S(2)}) async-start(bf16[8,18,2048]{2,1,0:T(8,128)(2,1)} %reshape.31), calls=%async_computation.1 | async-start | bytes 1572864 | tf_op jit(solution)/shard_map/all_to_all | solution.py:31
  95.0 104.8 %all-gather.2.cloned.1.call-start = ((), (), s32[]{:S(2)}) async-start(), calls=%async_computation.4 | async-start | bytes 5308416 | tf_op jit(solution)/shard_map/all_gather | solution.py:45
Sparse Core Ops, SparseCore 0:
  10.5 76.5 all-reduce.1
  125.7 74.1 all-gather.1
where the time goes:
time: 278 us; the launch traced here: 277 us
  blocking collectives  100 us (36%)
  waiting for transfers between devices  93.5 us (34%)
  matrix products  24.7 us (9%)
  other arithmetic  24.2 us (9%)
  between operations  14.2 us (5%)
  starting transfers between devices  11 us (4%)
  local copies, waits for them, and re-layouts  8.65 us (3%)
    psum x1, waiting for transfers between devices, per_device(): lax.psum(terms_in.astype(jnp.bfloat16), 'tp').astype(jnp.float32)  67.7 us
    all_to_all x1, blocking collectives, per_device(): lax.all_to_all(normed, 'dp', split_axis=1, concat_axis=0, tiled=True)  63.4 us
    pmax x1, blocking collectives, agree(): return lax.pmax(largest, ('dp', 'tp')) + 1e-06  37 us
    all_to_all x1, waiting for transfers between devices, per_device(): lax.all_to_all(outgoing, 'dp', split_axis=0, concat_axis=0, tiled=True)  17.2 us
    dot_general x1, matrix products, per_device(): jnp.einsum('dsr,dsc->drc', blocks, errors, preferred_element_type=jnp.flo...  16.4 us
    convert_element_type x1, other arithmetic, rounded_terms(): (partial_value / scale).astype(jnp.bfloat16)  11.1 us
    dot_general x1, matrix products, per_device(): pred = jnp.dot(normed, projection, preferred_element_type=jnp.float32)  8.38 us
    all_gather x1, waiting for transfers between devices, per_device(): lax.all_gather(diff, 'dp', axis=0, tiled=True)  7.88 us
  transfers between devices with their start and end apart: 4, of which 3 were waited for; matrix products, arithmetic and copies ran while one was open for 4% of the time, Pallas kernels for 0%

commit v1 on v0

v1 whole, which is shorter than its diff:
```python
import functools

import jax
import jax.numpy as jnp
from jax import lax
from jax.experimental import pallas as pl
from jax.experimental.pallas import tpu as pltpu
from jax.sharding import PartitionSpec as P

MESH = pl.DeviceIdType.MESH


def greet(groups):
    barrier = pltpu.get_barrier_semaphore()
    total = 0
    for axis, size in groups:
        me = lax.axis_index(axis)
        for step in range(1, size):
            pl.semaphore_signal(
                barrier, inc=1, device_id={axis: lax.rem(me + step, size)}, device_id_type=MESH
            )
        total += size - 1
    pl.semaphore_wait(barrier, total)


def remote(src, dst, send_sem, recv_sem, axis, target):
    return pltpu.make_async_remote_copy(
        src_ref=src,
        dst_ref=dst,
        send_sem=send_sem,
        recv_sem=recv_sem,
        device_id={axis: target},
        device_id_type=MESH,
    )


def exchange(axis, size, pick, dst, send_sem, recv_sem):
    me = lax.axis_index(axis)
    copies = []
    for step in range(1, size):
        peer = lax.rem(me + step, size)
        copies.append(
            remote(
                pick(peer), dst.at[me], send_sem.at[step], recv_sem.at[step], axis, peer
            )
        )
    return copies


def first_kernel(
    n, t, terms, blocks, index, terms_out, blocks_out, index_out,
    hold_terms, hold_blocks, hold_index, local_sem, t_send, t_recv, b_send, b_recv, i_send, i_recv,
):
    width = terms_out.shape[2]
    me_t, me_d = lax.axis_index("tp"), lax.axis_index("dp")

    def columns(peer):
        return terms.at[:, pl.ds(pl.multiple_of(peer * width, 128), width)]

    loads = [
        pltpu.make_async_copy(columns(me_t), hold_terms, local_sem.at[0]),
        pltpu.make_async_copy(blocks.at[me_d], hold_blocks, local_sem.at[1]),
        pltpu.make_async_copy(index.at[me_d], hold_index, local_sem.at[2]),
    ]
    for load in loads:
        load.start()
    greet((("tp", t), ("dp", n)))
    copies = exchange("tp", t, columns, terms_out, t_send, t_recv)
    copies += exchange("dp", n, lambda peer: index.at[peer], index_out, i_send, i_recv)
    copies += exchange("dp", n, lambda peer: blocks.at[peer], blocks_out, b_send, b_recv)
    for copy in copies:
        copy.start()
    stores = [
        pltpu.make_async_copy(hold_terms, terms_out.at[me_t], local_sem.at[3]),
        pltpu.make_async_copy(hold_blocks, blocks_out.at[me_d], local_sem.at[4]),
        pltpu.make_async_copy(hold_index, index_out.at[me_d], local_sem.at[5]),
    ]
    for load, store in zip(loads, stores):
        load.wait()
        store.start()
    for store in stores:
        store.wait()
    for copy in copies:
        copy.wait()


def rows_kernel(n, rows, rows_out, hold, local_sem, send, recv):
    me = lax.axis_index("dp")
    load = pltpu.make_async_copy(rows.at[me], hold, local_sem.at[0])
    load.start()
    greet((("dp", n),))
    copies = exchange("dp", n, lambda peer: rows.at[peer], rows_out, send, recv)
    for copy in copies:
        copy.start()
    load.wait()
    store = pltpu.make_async_copy(hold, rows_out.at[me], local_sem.at[1])
    store.start()
    store.wait()
    for copy in copies:
        copy.wait()


def last_kernel(
    n, t, pieces, diff, blocks, out,
    errors, partials, largest, mine_t, mine_d, from_t, from_d,
    local_sem, send, recv, mt_send, mt_recv, md_send, md_recv,
):
    me = lax.axis_index("dp")
    chip, core = me // 2, me % 2
    chips = n // 2
    other = 1 - core
    partner = chip * 2 + other
    width = errors.shape[3]
    features = out.shape[0]

    def piece(source, q, way, target):
        return remote(
            errors.at[source, q], errors.at[source, q],
            send.at[source, q, way], recv.at[source, q], "dp", target,
        )

    def local(q):
        return pltpu.make_async_copy(
            diff.at[:, pl.ds(pl.multiple_of(q * width, 128), width)],
            errors.at[me, q], local_sem.at[q],
        )

    for q in range(pieces):
        local(q).start()
    largest[...] = jnp.zeros_like(largest)
    greet((("tp", t), ("dp", n)))
    for q in range(pieces):
        local(q).wait()

        @pl.when(chip > 0)
        def _():
            piece(me, q, 0, me - 2).start()

        @pl.when(chip < chips - 1)
        def _():
            piece(me, q, 1, me + 2).start()

        piece(me, q, 2, partner).start()

    def compute(source, q):
        value = jnp.dot(blocks[source], errors[source, q], preferred_element_type=jnp.float32)
        partials[source, q] = value
        folded = jnp.max(jnp.abs(value).reshape(features // 8, 8, width), axis=0)
        largest[...] = jnp.maximum(largest[...], folded)

    @pl.loop(0, pieces)
    def _(q):
        compute(me, q)

    def arrive(i, _):
        step, q = i // pieces + 1, i % pieces
        left, right = me - 2 * step, me + 2 * step

        @pl.when(chip >= step)
        def _():
            piece(left, q, 1, partner).wait_recv()
            piece(left, q, 2, partner).start()

            @pl.when(chip < chips - 1)
            def _():
                piece(left, q, 1, me + 2).start()

        @pl.when(chip + step < chips)
        def _():
            piece(right, q, 0, partner).wait_recv()
            piece(right, q, 2, partner).start()

            @pl.when(chip > 0)
            def _():
                piece(right, q, 0, me - 2).start()

        @pl.when(chip >= step)
        def _():
            compute(left, q)

        @pl.when(chip + step < chips)
        def _():
            compute(right, q)

        return 0

    lax.fori_loop(0, (chips - 1) * pieces, arrive, 0)

    @pl.loop(0, chips * pieces)
    def _(i):
        source, q = (i // pieces) * 2 + other, i % pieces
        piece(source, q, 2, partner).wait_recv()
        compute(source, q)

    tile = mine_t.shape
    mine_t[...] = jnp.broadcast_to(jnp.max(largest[...]), tile)
    copies = exchange("tp", t, lambda peer: mine_t, from_t, mt_send, mt_recv)
    for copy in copies:
        copy.start()
    best = mine_t[...]
    for step in range(1, t):
        copies[step - 1].wait()
        best = jnp.maximum(best, from_t[lax.rem(lax.axis_index("tp") + t - step, t)])
    mine_d[...] = best
    copies = exchange("dp", n, lambda peer: mine_d, from_d, md_send, md_recv)
    for copy in copies:
        copy.start()
    for step in range(1, n):
        copies[step - 1].wait()
        best = jnp.maximum(best, from_d[lax.rem(me + n - step, n)])
    inverse = 1.0 / (jnp.max(best) + 1e-06)

    high = 16 if features % 16 == 0 else 8

    @pl.loop(0, features // high)
    def _(block):
        rows = pl.ds(pl.multiple_of(block * high, high), high)
        for q in range(pieces):
            total = jnp.zeros((high, width), jnp.float32)
            for source in range(n):
                term = (partials[source, q, rows, :] * inverse).astype(jnp.bfloat16)
                total = total + term.astype(jnp.float32)
            out[rows, pl.ds(q * width, width)] = total

    @pl.loop(0, chips * pieces)
    def _(i):
        source_chip, q = i // pieces, i % pieces
        source = source_chip * 2 + core
        piece(source, q, 2, partner).wait_send()

        @pl.when((source_chip >= chip) & (chip > 0))
        def _():
            piece(source, q, 0, me - 2).wait_send()

        @pl.when((source_chip <= chip) & (chip < chips - 1))
        def _():
            piece(source, q, 1, me + 2).wait_send()


def dma(*shape):
    return pltpu.SemaphoreType.DMA(shape)


def call(kernel, collective_id, operands, in_specs, out_shape, out_specs, scratch, flops=0):
    return pl.pallas_call(
        kernel,
        out_shape=out_shape,
        in_specs=in_specs,
        out_specs=out_specs,
        scratch_shapes=scratch,
        compiler_params=pltpu.CompilerParams(
            collective_id=collective_id, has_side_effects=True
        ),
    )(*operands)


def per_device(student_hidden, norm_gain, projection, teacher_partials, teacher_residual, owner):
    columns = projection.shape[1]
    rows_dev, features_all = student_hidden.shape
    n, t = lax.axis_size("dp"), lax.axis_size("tp")
    slots = rows_dev // n
    share = features_all // n
    wide = -(-share // 128) * 128
    hbm = pl.BlockSpec(memory_space=pl.ANY)
    vmem = pl.BlockSpec(memory_space=pltpu.VMEM)
    bf16, f32, i32 = jnp.bfloat16, jnp.float32, jnp.int32

    order = jnp.argsort(owner // rows_dev, stable=True)
    index = jnp.pad(owner[order].reshape(n, 1, slots), ((0, 0), (0, 0), (0, 128 - slots)))
    values = student_hidden.astype(f32)
    inverse = lax.rsqrt(jnp.mean(values * values, axis=-1, keepdims=True) + 1e-05)
    normed = (values * inverse * norm_gain).astype(bf16)
    blocks = jnp.pad(
        normed.reshape(rows_dev, n, share).transpose(1, 0, 2), ((0, 0), (0, 0), (0, wide - share))
    )
    terms, arrived_blocks, arrived_index = call(
        functools.partial(first_kernel, n, t), 0,
        (teacher_partials[0], blocks, index),
        [hbm] * 3,
        [
            jax.ShapeDtypeStruct((t, rows_dev, columns), bf16),
            jax.ShapeDtypeStruct((n, rows_dev, wide), bf16),
            jax.ShapeDtypeStruct((n, 1, 128), i32),
        ],
        [hbm] * 3,
        [
            pltpu.VMEM((rows_dev, columns), bf16),
            pltpu.VMEM((rows_dev, wide), bf16),
            pltpu.VMEM((1, 128), i32),
            dma(6), dma(t), dma(t), dma(n), dma(n), dma(n), dma(n),
        ],
    )
    summed = jnp.sum(terms.astype(f32), axis=0)
    teacher = (teacher_residual.astype(f32) + summed).astype(bf16)
    outgoing = teacher[order].reshape(n, slots, columns)
    arrived = call(
        functools.partial(rows_kernel, n), 1,
        (outgoing,),
        [hbm],
        jax.ShapeDtypeStruct((n, slots, columns), bf16),
        hbm,
        [pltpu.VMEM((slots, columns), bf16), dma(2), dma(n), dma(n)],
    )
    placing = jnp.argsort(arrived_index[:, 0, :slots].reshape(-1) % rows_dev)
    target = arrived.reshape(rows_dev, columns)[placing]
    pred = jnp.dot(normed, projection, preferred_element_type=f32)
    diff = (pred - target.astype(f32)).astype(bf16)
    turned = arrived_blocks[:, :, :share].transpose(0, 2, 1)
    pieces = 4 if columns % 512 == 0 and columns >= 2048 else 1
    width = columns // pieces
    return call(
        functools.partial(last_kernel, n, t, pieces), 2,
        (diff, turned),
        [hbm, vmem],
        jax.ShapeDtypeStruct((share, columns), f32),
        vmem,
        [
            pltpu.VMEM((n, pieces, rows_dev, width), bf16),
            pltpu.VMEM((n, pieces, share, width), f32),
            pltpu.VMEM((8, width), f32),
            pltpu.VMEM((8, 128), f32),
            pltpu.VMEM((8, 128), f32),
            pltpu.VMEM((t, 8, 128), f32),
            pltpu.VMEM((n, 8, 128), f32),
            dma(pieces), dma(n, pieces, 3), dma(n, pieces), dma(t), dma(t), dma(n), dma(n),
        ],
    )


def solution(mesh):
    placed = (P("dp", None), P(), P(None, "tp"), P("tp", "dp", None), P("dp", "tp"), P("dp"))
    return jax.shard_map(
        per_device, mesh=mesh, in_specs=placed, out_specs=P("dp", "tp"), check_vma=False
    )
```

time: 278 us -> 153 us (0.55)
  Pallas kernels: 0 us -> 115 us
  blocking collectives: 100 us -> 0 us
  waiting for transfers between devices: 93.5 us -> 0 us
  matrix products: 24.7 us -> 8.26 us
  between operations: 14.2 us -> 0.14 us
  other arithmetic: 24.2 us -> 11.4 us
  starting transfers between devices: 11 us -> 0 us
  local copies, waits for them, and re-layouts: 8.65 us -> 18.2 us
    pallas_call x0 -> x3, Pallas kernels: none -> 115 us  [call(): pl.pallas_call(kernel, out_shape=out_shape, in_specs=in_specs, out_specs=...]
    psum x1 -> x0, waiting for transfers between devices: 67.7 us -> none  [per_device(): lax.psum(terms_in.astype(jnp.bfloat16), 'tp').astype(jnp.float32)]
    all_to_all x1 -> x0, blocking collectives: 63.4 us -> none  [per_device(): lax.all_to_all(normed, 'dp', split_axis=1, concat_axis=0, tiled=True)]
    pmax x1 -> x0, blocking collectives: 37 us -> none  [agree(): return lax.pmax(largest, ('dp', 'tp')) + 1e-06]
    all_to_all x2 -> x0, waiting for transfers between devices: 17.2 us -> none  [the longest x1 17.2 us: per_device(): lax.all_to_all(outgoing, 'dp', split_axis=0, concat_axis=0, tiled=True)]
    dot_general x2 -> x1, matrix products: 24.7 us -> 8.26 us  [per_device(): pred = jnp.dot(normed, projection, preferred_element_type=f32)]
    convert_element_type x3 -> x2, other arithmetic: 12.6 us -> 0.42 us  [the longest x1 0.3 us: per_device(): normed = (values * inverse * norm_gain).astype(bf16)]
    all_to_all x2 -> x0, starting transfers between devices: 11 us -> none  [the longest x1 6.35 us: per_device(): lax.all_to_all(outgoing_owner, 'dp', split_axis=0, concat_axis=0, tiled=T...]
  transfers between devices with their start and end apart: 4 -> 0, of which waited for: 3 -> 0; matrix products, arithmetic and copies ran while one was open for 4% -> 0% of each run, Pallas kernels for 0% -> 0%
where the time goes in v1:
time: 153 us
  Pallas kernels  115 us (75%)
  local copies, waits for them, and re-layouts  18.2 us (12%)
  other arithmetic  11.4 us (7%)
  matrix products  8.26 us (5%)
    pallas_call x3, Pallas kernels, call(): pl.pallas_call(kernel, out_shape=out_shape, in_specs=in_specs, out_specs=...  115 us
    dot_general x1, matrix products, per_device(): pred = jnp.dot(normed, projection, preferred_element_type=f32)  8.26 us
    unnamed x11, local copies, waits for them, and re-layouts  4.22 us
    sort x1, other arithmetic, per_device(): placing = jnp.argsort(arrived_index[:, 0, :slots].reshape(-1) % rows_dev)  3.18 us
    sort x1, other arithmetic, per_device(): order = jnp.argsort(owner // rows_dev, stable=True)  3.17 us

profile of v1, /device:TPU:0, one launch (start us, length us, event | category | flops | bytes accessed | tf_op | source)
XLA Modules:
  0.0 153.1 jit_solution(1084507712129027238)
XLA Ops:
  0.0 1.6 %fusion.1 = f32[144]{0:T(256)S(1)} fusion(bf16[144,3456]{1,0:T(8,128)(2,1)} %param.6), kind=kLoop, calls=%fused_computation.8 | loop fusion | flops 1492848 | bytes 995904 | tf_op jit(solution)/shard_map/reduce_sum | solution.py:271
  1.6 0.7 and_select_fusion.1
  2.3 3.2 %sort.34 = (s32[144]{0:T(256)}, s32[144]{0:T(256)S(1)}) sort(s32[144]{0:T(256)S(1)} %and_select_fusion.1, s32[144]{0:T(256)S(1)} %iota.8), dimensions={0}, to_apply=%region_1.2 | sort | flops 1152 | bytes 2304 | tf_op jit(solution)/shard_map/jit(argsort)/sort | solution.py:268
  5.5 2.0 %gather_fusion = s32[144]{0:T(256)S(1)} fusion(s32[144]{0:T(256)} %param.11, s32[1024]{0:T(1024)S(1)} %pad_clamp_fusion.1), kind=kCustom, calls=%fused_computation | custom fusion | bytes 1728 | tf_op jit(solution)/shard_map/gather | solution.py:269
  7.5 0.1 reshape.24
  7.6 0.6 pad.9.index
  8.2 0.0 copy-done
  8.2 0.0 copy-done.3
  8.2 0.3 fusion.3
  8.5 2.7 %reshape.23 = bf16[144,8,432]{2,1,0:T(8,128)(2,1)S(1)} reshape(bf16[144,3456]{1,0:T(8,128)(2,1)S(1)} %fusion.3) | data formatting | bytes 1990656 | tf_op jit(solution)/shard_map/reshape | solution.py:274
  11.2 0.4 copy.11
  11.5 1.2 pad.8.blocks
  12.7 33.6 %shard_map.64 = (bf16[4,144,2048]{2,1,0:T(8,128)(2,1)}, bf16[8,144,512]{2,1,0:T(8,128)(2,1)}, s32[8,1,128]{2,1,0:T(1,128)}) custom-call(bf16[144,8192]{1,0:T(8,128)(2,1)} %bitcast.9, bf16[8,144,512]{2,1,0:T(8,128)(2,1)} %pad.8.blocks, s32[8,1,128]{2,1,0:T(1,128)} %pad.9.index), custom_call_target="tpu_custom_call" | custom-call | tf_op jit(solution)/shard_map/pallas_call | solution.py:245
  46.3 0.0 copy-start.2
  46.4 2.3 %convert_reduce_fusion = f32[144,2048]{1,0:T(8,128)S(1)} fusion(bf16[4,144,2048]{2,1,0:T(8,128)(2,1)} %get-tuple-element.11), kind=kLoop, calls=%fused_computation.3 | loop fusion | flops 2064384 | bytes 3538944 | tf_op jit(solution)/shard_map/reduce_sum | solution.py:293
  48.7 0.0 copy-done.2
  48.7 0.1 add_convert_fusion
  48.8 0.0 copy-start.4
  48.8 1.0 gather_fusion.1
  49.8 0.0 copy-done.4
  49.8 0.1 rem.23
  49.9 3.2 %sort.35 = (s32[144]{0:T(256)}, s32[144]{0:T(256)S(1)}) sort(s32[144]{0:T(256)S(1)} %and_select_fusion, s32[144]{0:T(256)S(1)} %iota.9), dimensions={0}, to_apply=%region_3.4 | sort | flops 1152 | bytes 2304 | tf_op jit(solution)/shard_map/jit(argsort)/sort | solution.py:304
  53.1 1.1 reshape.25.rows
  54.2 15.5 %shard_map.65 = bf16[8,18,2048]{2,1,0:T(8,128)(2,1)} custom-call(bf16[8,18,2048]{2,1,0:T(8,128)(2,1)} %reshape.25.rows), custom_call_target="tpu_custom_call" | custom-call | tf_op jit(solution)/shard_map/pallas_call | solution.py:245
  69.7 1.3 reshape.26
  71.0 1.0 gather_fusion.2
  72.0 0.0 copy-start.1
  72.0 8.3 %fusion.diff = bf16[144,2048]{1,0:T(8,128)(2,1)} fusion(bf16[144,3456]{1,0:T(8,128)(2,1)S(1)} %fusion.3, bf16[3456,2048]{1,0:T(8,128)(2,1)} %param.8, bf16[144,2048]{1,0:T(8,128)(2,1)S(1)} %gather_fusion.2), kind=kOutput, calls=%fused_computation.7 | convolution fusion | flops 2039316480 | bytes 16330752 | tf_op jit(solution)/shard_map/dot_general | solution.py:306
  80.3 1.4 copy.9
  81.7 1.3 slice_bitcast_fusion.blocks
  83.0 65.9 %shard_map.66 = f32[432,2048]{1,0:T(8,128)} custom-call(bf16[144,2048]{1,0:T(8,128)(2,1)} %fusion.diff, bf16[8,432,144]{2,1,0:T(8,128)(2,1)} %slice_bitcast_fusion.blocks), custom_call_target="tpu_custom_call" | custom-call | tf_op jit(solution)/shard_map/pallas_call | solution.py:245
  148.9 4.2 %copy.13 = f32[432,2048]{1,0:T(8,128)} copy(f32[432,2048]{1,0:T(8,128)} %shard_map.66) | data formatting | bytes 7077888
  (12 shorter events, 0.1 us)
Async XLA Ops:
  0.0 8.2 %copy-start = (bf16[144,3456]{1,0:T(8,128)(2,1)S(1)}, bf16[144,3456]{1,0:T(8,128)(2,1)}, u32[]{:S(2)}) copy-start(bf16[144,3456]{1,0:T(8,128)(2,1)} %param.6) | copy-start | bytes 2985988
  0.0 8.2 %copy-start.3 = (f32[3456]{0:T(1024)S(1)}, f32[3456]{0:T(1024)}, u32[]{:S(2)}) copy-start(f32[3456]{0:T(1024)} %param.7) | copy-start | bytes 41476
  46.3 2.3 %copy-start.2 = (bf16[144,2048]{1,0:T(8,128)(2,1)S(1)}, bf16[144,2048]{1,0:T(8,128)(2,1)}, u32[]{:S(2)}) copy-start(bf16[144,2048]{1,0:T(8,128)(2,1)} %param.10) | copy-start | bytes 1769476
  48.8 1.0 copy-start.4
  72.0 8.3 %copy-start.1 = (bf16[8,144,512]{2,1,0:T(8,128)(2,1)S(1)}, bf16[8,144,512]{2,1,0:T(8,128)(2,1)}, u32[]{:S(2)}) copy-start(bf16[8,144,512]{2,1,0:T(8,128)(2,1)} %get-tuple-element.14) | copy-start | bytes 3538948
